TPU v7x, 32 devices: a whole 2x2x4 slice. The times are simulated.
32 devices in a mesh: seq: 16 (over z, x, core), tp: 2 (over y).
Axes of the slice: x: 2, y: 2, z: 4, core: 2. Of those that a mesh axis runs over, the one named last changes fastest.
Arguments:
- tokens: bfloat16 [256, 8192], P('tp', 'seq'), may hold values from -6 to 6
- gate_weight: bfloat16 [8192, 14336], P('seq', 'tp'), may hold values from -0.0625 to 0.0625
- up_weight: bfloat16 [8192, 14336], P('seq', 'tp'), may hold values from -0.0625 to 0.0625
- down_weight: bfloat16 [14336, 8192], P('tp', 'seq'), may hold values from -0.09375 to 0.09375
- masks: int32 [2, 112], P(None, 'tp'), may hold values from 0 to 1, as said below
- cotangent: bfloat16 [256, 8192], P('tp', 'seq'), may hold values from -6 to 6
Outputs:
- output: bfloat16 [256, 8192], P('tp', 'seq')
- grad_tokens: bfloat16 [256, 8192], P('tp', 'seq')
- grad_gate: float32 [8192, 14336], P('seq', 'tp')
- grad_up: float32 [8192, 14336], P('seq', 'tp')
- grad_down: float32 [14336, 8192], P('tp', 'seq')
Inputs may be any that keep to these rules, and one draw needn't show every extreme that they name: Each row of masks holds exactly 28 ones. Cut a row into 2 groups of 56 consecutive blocks: in every row one group holds exactly 28 ones, and the remaining ones are spread over the other groups as evenly as possible, so that their counts differ by at most one.
All inputs are finite; a program needn't handle non-finite values.
Results may differ from a plain program's by a relative error of at most 0.0049.
Values may be sent and summed in bfloat16 or wider, within the bound.
A program may use at most 192 MiB of HBM per device.

v0:
```python
import math

import jax
import jax.numpy as jnp
from jax import lax
from jax.sharding import PartitionSpec as P

FF = 14336
BLK = 128
ROWBLK = 128


def slot_tables(mask_local, capacity):
    running_total = jnp.cumsum(mask_local, axis=1) - 1
    slot_ids = jnp.arange(capacity, dtype=jnp.int32)
    block_ids = jnp.arange(mask_local.shape[1], dtype=jnp.int32)
    slot_hit = (mask_local[:, None, :] == 1) & (
        running_total[:, None, :] == slot_ids[None, :, None]
    )
    slot_indicator = slot_hit.astype(jnp.float32)
    slot_block = jnp.sum(jnp.where(slot_hit, block_ids[None, None, :], 0), axis=2)
    slot_live = jnp.sum(slot_indicator, axis=2)
    return (slot_indicator, slot_block, slot_live)


def rows_live(slot_live, row_start, row_count):
    row_block = (row_start + jnp.arange(row_count, dtype=jnp.int32)) // ROWBLK
    select = (
        row_block[:, None] == jnp.arange(slot_live.shape[0], dtype=jnp.int32)[None, :]
    ).astype(jnp.float32)
    live = jnp.dot(select, slot_live, preferred_element_type=jnp.float32)
    return jnp.repeat(live, BLK, axis=1)


def shards(tokens, gate_weight, up_weight, down_weight, masks, cotangent):
    seq_count = lax.axis_size("seq")
    tp_count = lax.axis_size("tp")
    all_rows, grad_rows = (
        lax.all_gather(tokens, "tp", axis=0, tiled=True),
        lax.all_gather(cotangent, "tp", axis=0, tiled=True),
    )
    total_row_count = all_rows.shape[0]
    feat_cols = all_rows.shape[1]
    local_blocks = masks.shape[1]
    row_blocks = total_row_count // ROWBLK
    kept_total = FF // BLK // 4
    capacity = 2 * kept_total // tp_count
    packed_cols = capacity * BLK
    slot_indicator, slot_block, slot_live = slot_tables(masks, capacity)
    gate_blocks = jnp.take(gate_weight.reshape(feat_cols, local_blocks, BLK), slot_block, axis=1)
    up_blocks = jnp.take(up_weight.reshape(feat_cols, local_blocks, BLK), slot_block, axis=1)
    down_blocks = jnp.take(down_weight.reshape(local_blocks, BLK, feat_cols), slot_block, axis=0)
    token_blocks = all_rows.reshape(row_blocks, ROWBLK, feat_cols)
    gate_part = jnp.einsum(
        "rtd,drck->rtck", token_blocks, gate_blocks, preferred_element_type=jnp.float32
    ).reshape(total_row_count, packed_cols)
    up_part = jnp.einsum(
        "rtd,drck->rtck", token_blocks, up_blocks, preferred_element_type=jnp.float32
    ).reshape(total_row_count, packed_cols)
    own_rows = total_row_count // seq_count
    own_start = lax.axis_index("seq") * own_rows
    local_live_blocks = rows_live(slot_live, own_start, own_rows)
    gate_all, up_all = lax.psum((gate_part, up_part), "seq")
    every_live = rows_live(slot_live, 0, total_row_count)
    hidden = (jax.nn.silu(gate_all) * up_all * every_live).astype(jnp.bfloat16)
    gate_own = lax.dynamic_slice_in_dim(gate_all, own_start, own_rows, 0)
    up_own = lax.dynamic_slice_in_dim(up_all, own_start, own_rows, 0)
    hidden_blocks = hidden.reshape(row_blocks, ROWBLK, capacity, BLK)
    output_part = jnp.einsum(
        "rtck,rckd->rtd", hidden_blocks, down_blocks, preferred_element_type=jnp.float32
    ).reshape(total_row_count, feat_cols)
    output = lax.psum_scatter(output_part, "tp", scatter_dimension=0, tiled=True).astype(
        jnp.bfloat16
    )
    grad_blocks = grad_rows.reshape(row_blocks, ROWBLK, feat_cols)
    hidden_part = jnp.einsum(
        "rtd,rckd->rtck", grad_blocks, down_blocks, preferred_element_type=jnp.float32
    ).reshape(total_row_count, packed_cols)
    grad_hidden = (
        lax.psum_scatter(hidden_part, "seq", scatter_dimension=0, tiled=True) * local_live_blocks
    )
    sigmoid_gate = jax.nn.sigmoid(gate_own)
    grad_gate_own = (
        grad_hidden * up_own * sigmoid_gate * (1.0 + gate_own * (1.0 - sigmoid_gate))
    ).astype(jnp.bfloat16)
    grad_up_own = (grad_hidden * gate_own * sigmoid_gate).astype(jnp.bfloat16)
    grad_gate_act, grad_up_act = (
        lax.all_gather(grad_gate_own, "seq", axis=0, tiled=True),
        lax.all_gather(grad_up_own, "seq", axis=0, tiled=True),
    )
    grad_scale = 1.0 / math.sqrt(total_row_count)
    gate_act_blocks = grad_gate_act.reshape(row_blocks, ROWBLK, capacity, BLK)
    up_act_blocks = grad_up_act.reshape(row_blocks, ROWBLK, capacity, BLK)
    down_compact = jnp.einsum(
        "rtck,rtd->rckd", hidden_blocks, grad_blocks, preferred_element_type=jnp.float32
    )
    grad_down = jnp.einsum(
        "toh,toye->hye", slot_indicator, down_compact, precision=lax.Precision.HIGHEST
    )
    grad_down = grad_down.reshape(local_blocks * BLK, feat_cols) * grad_scale
    gate_packed = jnp.einsum(
        "rtd,rtck->drck", token_blocks, gate_act_blocks, preferred_element_type=jnp.float32
    )
    grad_gate = jnp.einsum(
        "rcb,drck->dbk", slot_indicator, gate_packed, precision=lax.Precision.HIGHEST
    )
    grad_gate = grad_gate.reshape(feat_cols, local_blocks * BLK) * grad_scale
    up_packed = jnp.einsum(
        "rtd,rtck->drck", token_blocks, up_act_blocks, preferred_element_type=jnp.float32
    )
    grad_up = jnp.einsum(
        "rcb,drck->dbk", slot_indicator, up_packed, precision=lax.Precision.HIGHEST
    )
    grad_up = grad_up.reshape(feat_cols, local_blocks * BLK) * grad_scale
    input_part = jnp.einsum(
        "rtck,drck->rtd", gate_act_blocks, gate_blocks, preferred_element_type=jnp.float32
    ) + jnp.einsum("rtck,drck->rtd", up_act_blocks, up_blocks, preferred_element_type=jnp.float32)
    input_part = input_part.reshape(total_row_count, feat_cols)
    grad_tokens = lax.psum_scatter(input_part, "tp", scatter_dimension=0, tiled=True).astype(
        jnp.bfloat16
    )
    return (output, grad_tokens, grad_gate, grad_up, grad_down)


def solution(mesh):
    placed = (
        P("tp", "seq"),
        P("seq", "tp"),
        P("seq", "tp"),
        P("tp", "seq"),
        P(None, "tp"),
        P("tp", "seq"),
    )
    return jax.shard_map(
        shards,
        mesh=mesh,
        in_specs=placed,
        out_specs=(P("tp", "seq"), P("tp", "seq"), P("seq", "tp"), P("seq", "tp"), P("tp", "seq")),
        check_vma=False,
    )
```

profile of v0, /device:TPU:0, one launch (start us, length us, event | category | flops | bytes accessed | tf_op | source)
XLA Modules:
  0.0 571.6 jit_solution(6944934957034259550)
XLA Ops:
  8.9 7.4 %all_gather.12 = bf16[256,512]{1,0:T(8,128)(2,1)S(1)} all-gather(bf16[128,512]{1,0:T(8,128)(2,1)} %param.8), channel_id=1, replica_groups=mesh['seq'=16,'tp'=2] {'tp'}, dimensions={0}, use_global_device_ids=true | all-gather | bytes 393216 | tf_op jit(solution)/shard_map/all_gather | solution.py:39
  16.4 10.4 %copy.75 = bf16[512,7168]{0,1:T(8,128)(2,1)} copy(bf16[512,7168]{1,0:T(8,128)(2,1)} %param.10) | data formatting | bytes 14680064 | tf_op args[2]
  26.8 10.4 %copy.76 = bf16[512,56,128]{2,0,1:T(8,128)(2,1)} copy(bf16[512,56,128]{0,2,1:T(8,128)(2,1)} %bitcast.128) | data formatting | bytes 14680064 | tf_op jit(solution)/shard_map/reshape | solution.py:51
  37.2 8.4 %gather_fusion.2 = bf16[56,512,128]{2,1,0:T(8,128)(2,1)} fusion(bf16[512,56,128]{2,0,1:T(8,128)(2,1)} %copy.76, s32[1024]{0:T(1024)S(1)} %pad_clamp_fusion.1), kind=kCustom, calls=%fused_computation.1.clone | custom fusion | bytes 14680288 | tf_op jit(solution)/shard_map/jit(_take)/gather | solution.py:51
  45.7 8.0 %fusion.24 = f32[2,128,28,128]{1,3,2,0:T(8,128)} fusion(bf16[2,128,512,1]{2,1,3,0:T(8,128)(2,1)S(1)} %bitcast.145, bf16[2,28,512,128]{3,2,1,0:T(8,128)(2,1)} %bitcast.138, pred[2,28]{1,0:T(4,128)(4,1)S(1)} %compare_and_fusion), kind=kOutput, calls=%fused_computation.37 | convolution fusion | flops 943194112 | bytes 11272248 | tf_op jit(solution)/shard_map/rtd,drck->rtck/dot_general | solution.py:57
  59.1 10.4 %copy.70 = bf16[512,7168]{0,1:T(8,128)(2,1)} copy(bf16[512,7168]{1,0:T(8,128)(2,1)} %param.9) | data formatting | bytes 14680064 | tf_op args[1]
  69.5 10.4 %copy.71 = bf16[512,56,128]{2,0,1:T(8,128)(2,1)} copy(bf16[512,56,128]{0,2,1:T(8,128)(2,1)} %bitcast.129) | data formatting | bytes 14680064 | tf_op jit(solution)/shard_map/reshape | solution.py:50
  79.9 8.3 %gather_fusion.1 = bf16[56,512,128]{2,1,0:T(8,128)(2,1)} fusion(bf16[512,56,128]{2,0,1:T(8,128)(2,1)} %copy.71, s32[1024]{0:T(1024)S(1)} %pad_clamp_fusion.1), kind=kCustom, calls=%fused_computation.clone | custom fusion | bytes 14680288 | tf_op jit(solution)/shard_map/jit(_take)/gather | solution.py:50
  88.3 8.0 %fusion.21 = f32[2,128,28,128]{1,3,2,0:T(8,128)} fusion(bf16[2,128,512,1]{2,1,3,0:T(8,128)(2,1)S(1)} %bitcast.146, bf16[2,28,512,128]{3,2,1,0:T(8,128)(2,1)} %bitcast.140, pred[2,28]{1,0:T(4,128)(4,1)S(1)} %compare_and_fusion), kind=kOutput, calls=%fused_computation.36 | convolution fusion | flops 943194112 | bytes 11272248 | tf_op jit(solution)/shard_map/rtd,drck->rtck/dot_general | solution.py:54
  101.8 13.5 %copy_bitcast_fusion.3 = (f32[256,3584]{1,0:T(8,128)}, f32[256,3584]{1,0:T(8,128)}) fusion(f32[32,8,28,128]{3,2,1,0:T(8,128)} %bitcast.131, f32[32,8,28,128]{3,2,1,0:T(8,128)} %bitcast.132), kind=kLoop, calls=%fused_computation.26 | loop fusion | bytes 14680064 | tf_op jit(solution)/shard_map/reshape | solution.py:59
  115.5 8.7 %gather_fusion = bf16[56,128,512]{2,1,0:T(8,128)(2,1)} fusion(bf16[56,128,512]{2,1,0:T(8,128)(2,1)} %bitcast.142, s32[1024]{0:T(1024)S(1)} %pad_clamp_fusion), kind=kCustom, calls=%fused_computation.2 | custom fusion | bytes 14680288 | tf_op jit(solution)/shard_map/jit(_take)/gather | solution.py:52
  129.8 7.2 %fusion.20 = f32[2,128,28,128]{1,3,2,0:T(8,128)} fusion(bf16[2,128,512,1]{2,1,3,0:T(8,128)(2,1)S(1)} %bitcast.149, bf16[2,28,128,512]{3,2,1,0:T(8,128)(2,1)} %bitcast.143, pred[2,28]{1,0:T(4,128)(4,1)S(1)} %compare_and_fusion), kind=kOutput, calls=%fused_computation.35 | convolution fusion | flops 943194112 | bytes 11272248 | tf_op jit(solution)/shard_map/rtd,rckd->rtck/dot_general | solution.py:76
  137.0 5.8 %copy.121 = f32[2,128,28,128]{3,2,1,0:T(8,128)} copy(f32[2,128,28,128]{1,3,2,0:T(8,128)} %fusion.20) | data formatting | bytes 7340032
  142.8 7.4 %copy.145 = f32[32,8,28,128]{3,1,2,0:T(8,128)} copy(f32[32,8,28,128]{3,2,1,0:T(8,128)} %bitcast.130) | data formatting | bytes 7340032
  158.0 113.9 %all-reduce.3.cloned.1.call-done = (f32[256,3584]{1,0:T(8,128)}, f32[256,3584]{1,0:T(8,128)}) async-done(((f32[256,3584]{1,0:T(8,128)}, f32[256,3584]{1,0:T(8,128)}), (f32[256,3584]{1,0:T(8,128)}, f32[256,3584]{1,0:T(8,128)})) %all-reduce.3.cloned.1.call-update) | async-done | bytes 7340048 | tf_op jit(solution)/shard_map/psum | solution.py:63
  271.9 6.6 %multiply_convert_fusion = bf16[256,3584]{1,0:T(8,128)(2,1)} fusion(f32[256,3584]{1,0:T(8,128)} %copy.80, f32[256,3584]{1,0:T(8,128)} %get-tuple-element.6, f32[256,3584]{1,0:T(8,128)} %get-tuple-element.7), kind=kLoop, calls=%fused_computation.34 | loop fusion | flops 6422528 | bytes 12845056 | tf_op jit(solution)/shard_map/convert_element_type | solution.py:65
  284.3 6.3 %fusion.13 = f32[2,128,512,1]{2,1,3,0:T(8,128)} fusion(bf16[2,128,28,128]{1,3,2,0:T(8,128)(2,1)} %copy.93, bf16[2,28,128,512]{3,2,1,0:T(8,128)(2,1)} %bitcast.144, pred[2,28]{1,0:T(4,128)(4,1)S(1)} %compare_and_fusion), kind=kOutput, calls=%fused_computation.22 | convolution fusion | flops 943194112 | bytes 9699384 | tf_op jit(solution)/shard_map/rtck,rckd->rtd/dot_general | solution.py:69
  290.8 53.5 %reduce-scatter.10.cloned.1.call-done = f32[16,3584]{1,0:T(8,128)} async-done(((f32[256,3584]{1,0:T(8,128)}), f32[16,3584]{1,0:T(8,128)}) %reduce-scatter.10.cloned.1.call-update) | async-done | bytes 229392 | tf_op jit(solution)/shard_map/reduce_scatter | solution.py:80
  349.2 18.3 %bitcast_multiply_fusion = f32[56,128,512]{2,0,1:T(8,128)} fusion(f32[2,28,128,512]{3,2,1,0:T(8,128)S(1)} %fusion.57, s32[2,56]{1,0:T(2,128)S(1)} %broadcast_add_fusion, pred[2,56]{1,0:T(4,128)(4,1)S(1)} %broadcast_compare_fusion), kind=kOutput, calls=%fused_computation.7 | convolution fusion | flops 2469926912 | bytes 29360688 | tf_op jit(solution)/shard_map/toh,toye->hye/dot_general | solution.py:97
  367.5 19.3 %copy.95 = f32[56,128,512]{2,1,0:T(8,128)} copy(f32[56,128,512]{2,0,1:T(8,128)} %bitcast_multiply_fusion) | data formatting | bytes 29360128 | tf_op jit(solution)/shard_map/mul | solution.py:100
  388.4 14.5 %all-gather.3.cloned.1.call-done = bf16[256,3584]{1,0:T(8,128)(2,1)} async-done(((bf16[16,3584]{1,0:T(8,128)(2,1)}), bf16[256,3584]{1,0:T(8,128)(2,1)}) %all-gather.3.cloned.1.call-update) | async-done | bytes 1835024 | tf_op jit(solution)/shard_map/all_gather | solution.py:88
  409.1 6.4 %fusion.27 = f32[2,128,512]{2,1,0:T(8,128)S(1)} fusion(bf16[2,128,28,128]{1,3,2,0:T(8,128)(2,1)} %copy.89, bf16[2,28,512,128]{3,2,1,0:T(8,128)(2,1)} %bitcast.141, pred[2,28]{1,0:T(4,128)(4,1)S(1)} %compare_and_fusion), kind=kOutput, calls=%fused_computation.38 | convolution fusion | flops 943194112 | bytes 9699384 | tf_op jit(solution)/shard_map/rtck,drck->rtd/dot_general | solution.py:115
  415.5 7.5 %convolution_bitcast_fusion.1 = f32[512,2,28,128]{0,3,2,1:T(8,128)} fusion(bf16[2,128,28,128]{1,3,2,0:T(8,128)(2,1)S(1)} %copy-done.2, bf16[2,128,512,1]{2,1,3,0:T(8,128)(2,1)S(1)} %bitcast.147), kind=kOutput, calls=%fused_computation.24 | convolution fusion | flops 939524096 | bytes 16777216 | tf_op jit(solution)/shard_map/rtd,rtck->drck/dot_general | solution.py:101
  423.0 22.1 %all-gather.5.cloned.1.call-done = bf16[256,3584]{1,0:T(8,128)(2,1)} async-done(((bf16[16,3584]{1,0:T(8,128)(2,1)}), bf16[256,3584]{1,0:T(8,128)(2,1)}) %all-gather.5.cloned.1.call-update) | async-done | bytes 1835024 | tf_op jit(solution)/shard_map/all_gather | solution.py:89
  450.9 7.0 %fusion.33 = f32[2,128,512]{2,1,0:T(8,128)} fusion(f32[2,128,512]{2,1,0:T(8,128)S(1)} %fusion.27, bf16[2,128,28,128]{1,3,2,0:T(8,128)(2,1)} %copy.91, bf16[2,28,512,128]{3,2,1,0:T(8,128)(2,1)} %bitcast.139, pred[2,28]{1,0:T(4,128)(4,1)S(1)} %compare_and_fusion), kind=kOutput, calls=%fused_computation.40 | convolution fusion | flops 943325184 | bytes 10223672 | tf_op jit(solution)/shard_map/rtck,drck->rtd/dot_general | solution.py:117
  457.9 20.0 %copy.90 = f32[512,2,28,128]{3,2,1,0:T(8,128)} copy(f32[512,2,28,128]{0,3,2,1:T(8,128)} %convolution_bitcast_fusion.1) | data formatting | bytes 29360128 | tf_op jit(solution)/shard_map/rtd,rtck->drck/transpose | solution.py:101
  477.9 15.1 %bitcast_multiply_fusion.2 = f32[512,128,56]{1,2,0:T(8,128)} fusion(f32[512,2,28,128]{3,2,1,0:T(8,128)} %copy.90, s32[2,56]{1,0:T(2,128)S(1)} %broadcast_add_fusion, pred[2,56]{1,0:T(4,128)(4,1)S(1)} %broadcast_compare_fusion), kind=kOutput, calls=%fused_computation.9 | convolution fusion | flops 2469926912 | bytes 29360688 | tf_op jit(solution)/shard_map/rcb,drck->dbk/dot_general | solution.py:104
  493.1 7.3 %convolution_bitcast_fusion = f32[512,2,28,128]{0,3,2,1:T(8,128)} fusion(bf16[2,128,28,128]{1,3,2,0:T(8,128)(2,1)S(1)} %copy-done.1, bf16[2,128,512,1]{2,1,3,0:T(8,128)(2,1)S(1)} %bitcast.148), kind=kOutput, calls=%fused_computation.23 | convolution fusion | flops 939524096 | bytes 16777216 | tf_op jit(solution)/shard_map/rtd,rtck->drck/dot_general | solution.py:108
  500.3 13.8 %copy.144 = f32[64,8,56,128]{3,1,2,0:T(8,128)} copy(f32[64,8,56,128]{3,2,1,0:T(8,128)} %bitcast.126) | data formatting | bytes 29360128
  514.2 19.9 %copy.92 = f32[512,2,28,128]{3,2,1,0:T(8,128)} copy(f32[512,2,28,128]{0,3,2,1:T(8,128)} %convolution_bitcast_fusion) | data formatting | bytes 29360128 | tf_op jit(solution)/shard_map/rtd,rtck->drck/transpose | solution.py:108
  534.1 15.0 %bitcast_multiply_fusion.1 = f32[512,128,56]{1,2,0:T(8,128)} fusion(f32[512,2,28,128]{3,2,1,0:T(8,128)} %copy.92, s32[2,56]{1,0:T(2,128)S(1)} %broadcast_add_fusion, pred[2,56]{1,0:T(4,128)(4,1)S(1)} %broadcast_compare_fusion), kind=kOutput, calls=%fused_computation.8 | convolution fusion | flops 2469926912 | bytes 29360688 | tf_op jit(solution)/shard_map/rcb,drck->dbk/dot_general | solution.py:111
  549.1 13.8 %copy.143 = f32[64,8,56,128]{3,1,2,0:T(8,128)} copy(f32[64,8,56,128]{3,2,1,0:T(8,128)} %bitcast.127) | data formatting | bytes 29360128
  (54 shorter events, 52.5 us)
Async XLA Ops:
  7.2 264.7 %all-reduce.3.cloned.1.call-start = ((), (), s32[]{:S(2)}) async-start(), calls=%async_computation.8 | async-start | bytes 14680064 | tf_op jit(solution)/shard_map/psum | solution.py:63
  115.3 229.0 %reduce-scatter.10.cloned.1.call-start = ((), (), s32[]{:S(2)}) async-start(), calls=%async_computation.7 | async-start | bytes 3899392 | tf_op jit(solution)/shard_map/reduce_scatter | solution.py:80
  115.5 8.7 %copy-start.3 = (bf16[128,512]{1,0:T(8,128)(2,1)S(1)}, bf16[128,512]{1,0:T(8,128)(2,1)}, u32[]{:S(2)}) copy-start(bf16[128,512]{1,0:T(8,128)(2,1)} %param.13) | copy-start | bytes 393220
  150.3 236.4 %reduce-scatter.6.cloned.1.call-start = ((), (), s32[]{:S(2)}) async-start(), calls=%async_computation.3 | async-start | bytes 786432 | tf_op jit(solution)/shard_map/reduce_scatter | solution.py:72
  284.3 62.9 %copy-start = (bf16[2,128,28,128]{1,3,2,0:T(8,128)(2,1)S(1)}, bf16[2,128,28,128]{1,3,2,0:T(8,128)(2,1)}, u32[]{:S(2)}) copy-start(bf16[2,128,28,128]{1,3,2,0:T(8,128)(2,1)} %copy.93) | copy-start | bytes 5505028
  290.6 112.3 %all-gather.3.cloned.1.call-start = ((), (), s32[]{:S(2)}) async-start(), calls=%async_computation.4 | async-start | bytes 1949696 | tf_op jit(solution)/shard_map/all_gather | solution.py:88
  346.5 98.6 %all-gather.5.cloned.1.call-start = ((), (), s32[]{:S(2)}) async-start(), calls=%async_computation.5 | async-start | bytes 1949696 | tf_op jit(solution)/shard_map/all_gather | solution.py:89
  347.1 215.8 %reduce-scatter.8.cloned.1.call-start = ((), (), s32[]{:S(2)}) async-start(), calls=%async_computation.6 | async-start | bytes 786432 | tf_op jit(solution)/shard_map/reduce_scatter | solution.py:119
  409.0 6.4 %copy-start.2 = (bf16[2,128,28,128]{1,3,2,0:T(8,128)(2,1)S(1)}, bf16[2,128,28,128]{1,3,2,0:T(8,128)(2,1)}, u32[]{:S(2)}) copy-start(bf16[2,128,28,128]{1,3,2,0:T(8,128)(2,1)} %copy.89) | copy-start | bytes 5505028
  477.9 15.1 %copy-start.1 = (bf16[2,128,28,128]{1,3,2,0:T(8,128)(2,1)S(1)}, bf16[2,128,28,128]{1,3,2,0:T(8,128)(2,1)}, u32[]{:S(2)}) copy-start(bf16[2,128,28,128]{1,3,2,0:T(8,128)(2,1)} %copy.91) | copy-start | bytes 5505028
Sparse Core Ops, SparseCore 0:
  115.4 156.4 all-reduce.2
  275.7 68.5 reduce-scatter.9
  346.6 13.5 reduce-scatter.5
  362.3 40.5 all-gather.2
  405.6 39.4 all-gather.4
  458.0 13.4 reduce-scatter.7
where the time goes:
time: 582 us; the launch traced here: 572 us
  local copies, waits for them, and re-layouts  217 us (37%)
  waiting for transfers between devices  205 us (35%)
  matrix products  109 us (19%)
  between operations  14.5 us (2%)
  other arithmetic  13.7 us (2%)
  blocking collectives  13 us (2%)
    psum x1, waiting for transfers between devices, shards(): gate_all, up_all = lax.psum((gate_part, up_part), 'seq')  114 us
    unnamed x14, local copies, waits for them, and re-layouts  61.8 us
    reduce_scatter x1, waiting for transfers between devices, shards(): lax.psum_scatter(hidden_part, 'seq', scatter_dimension=0, tiled=True)  53.5 us
    all_gather x1, waiting for transfers between devices, shards(): lax.all_gather(grad_up_own, 'seq', axis=0, tiled=True)  22.1 us
    transpose x1, local copies, waits for them, and re-layouts, shards(): jnp.einsum('rtd,rtck->drck', token_blocks, gate_act_blocks, preferred_ele...  20 us
    transpose x1, local copies, waits for them, and re-layouts, shards(): jnp.einsum('rtd,rtck->drck', token_blocks, up_act_blocks, preferred_eleme...  19.9 us
    mul x1, local copies, waits for them, and re-layouts, shards(): grad_down = grad_down.reshape(local_blocks * BLK, feat_cols) * grad_scale  19.3 us
    reshape x2, local copies, waits for them, and re-layouts, shards(): up_part = jnp.einsum('rtd,drck->rtck', token_blocks, up_blocks, preferred...  19 us
  transfers between devices with their start and end apart: 6, of which 4 were waited for; matrix products, arithmetic and copies ran while one was open for 39% of the time, Pallas kernels for 0%

commit v1 on v0

v1 whole, which is shorter than its diff:
```python
import functools
import math

import jax
import jax.numpy as jnp
from jax import lax
from jax.experimental import pallas as pl
from jax.experimental.pallas import tpu as pltpu
from jax.sharding import PartitionSpec as P

BLK = 128
ROWBLK = 128
KEEP_PART = 4
MESH = pl.DeviceIdType.MESH
VMEM_LIMIT = 60 * 1024 * 1024


def group_of(count):
    for size in (7, 8, 4, 2):
        if count % size == 0:
            return size
    return 1


def tables_kernel(mask_ref, block_ref, live_ref, slot_ref):
    row_blocks, blocks = mask_ref.shape
    capacity = block_ref.shape[1]
    for row in range(row_blocks):
        for slot in range(capacity):
            block_ref[row, slot] = 0
            live_ref[row, slot] = 0

        def step(block, taken, row=row):
            kept = mask_ref[row, block]
            at = jnp.minimum(taken, capacity - 1)
            slot_ref[row, block] = at

            @pl.when(kept == 1)
            def _():
                block_ref[row, at] = block
                live_ref[row, at] = 1

            return taken + kept

        lax.fori_loop(0, blocks, step, jnp.int32(0))


def slot_tables(masks, capacity):
    row_blocks, blocks = masks.shape
    smem = pl.BlockSpec(memory_space=pltpu.SMEM)
    return pl.pallas_call(
        tables_kernel,
        out_shape=(
            jax.ShapeDtypeStruct((row_blocks, capacity), jnp.int32),
            jax.ShapeDtypeStruct((row_blocks, capacity), jnp.int32),
            jax.ShapeDtypeStruct((row_blocks, blocks), jnp.int32),
        ),
        in_specs=[smem],
        out_specs=(smem, smem, smem),
    )(masks)


def rows_kernel(count, tok_ref, cot_ref, tok_all, cot_all, send_sem, recv_sem, own_sem):
    me = lax.axis_index("tp")
    barrier = pltpu.get_barrier_semaphore()
    for shift in range(1, count):
        pl.semaphore_signal(
            barrier, inc=1, device_id={"tp": lax.rem(me + shift, count)}, device_id_type=MESH
        )
    pl.semaphore_wait(barrier, count - 1)
    copies = []
    for which, (src, dst) in enumerate(((tok_ref, tok_all), (cot_ref, cot_all))):
        for shift in range(1, count):
            copy = pltpu.make_async_remote_copy(
                src_ref=src,
                dst_ref=dst.at[me],
                send_sem=send_sem.at[which, shift],
                recv_sem=recv_sem.at[which, shift],
                device_id={"tp": lax.rem(me + shift, count)},
                device_id_type=MESH,
            )
            copy.start()
            copies.append(copy)
        own = pltpu.make_async_copy(src, dst.at[me], own_sem.at[which])
        own.start()
        copies.append(own)
    for copy in copies:
        copy.wait()


def gather_rows(tokens, cotangent):
    count = lax.axis_size("tp")
    rows, feats = tokens.shape
    anywhere = pl.BlockSpec(memory_space=pl.ANY)
    return pl.pallas_call(
        functools.partial(rows_kernel, count),
        out_shape=(jax.ShapeDtypeStruct((count, rows, feats), tokens.dtype),) * 2,
        in_specs=[anywhere] * 2,
        out_specs=(anywhere,) * 2,
        scratch_shapes=[
            pltpu.SemaphoreType.DMA((2, count)),
            pltpu.SemaphoreType.DMA((2, count)),
            pltpu.SemaphoreType.DMA((2,)),
        ],
        compiler_params=pltpu.CompilerParams(collective_id=0, has_side_effects=True),
    )(tokens, cotangent)


def parts_kernel(group, block_ref, live_ref, tok_ref, cot_ref, *refs):
    gates, ups, downs = refs[:group], refs[group : 2 * group], refs[2 * group : 3 * group]
    out_ref = refs[3 * group]
    row, step = pl.program_id(0), pl.program_id(1)
    tok, cot = tok_ref[...], cot_ref[...]
    owners, _, own_rows, _ = out_ref.shape
    for at in range(group):
        live = live_ref[row, step * group + at] == 1
        columns = slice(at * BLK, (at + 1) * BLK)
        gate = jnp.dot(tok, gates[at][...], preferred_element_type=jnp.float32)
        up = jnp.dot(tok, ups[at][...], preferred_element_type=jnp.float32)
        grad = lax.dot_general(
            cot, downs[at][...], (((1,), (1,)), ((), ())), preferred_element_type=jnp.float32
        )
        up = jnp.where(live, up, 0.0)
        grad = jnp.where(live, grad, 0.0)
        for which, value in enumerate((gate, up, grad)):
            out_ref[:, which, :, columns] = value.reshape(owners, own_rows, BLK)


def weight_specs(group, feats):
    def columns(at):
        return pl.BlockSpec(
            (feats, BLK), lambda row, step, block, live: (0, block[row, step * group + at])
        )

    def rows(at):
        return pl.BlockSpec(
            (BLK, feats), lambda row, step, block, live: (block[row, step * group + at], 0)
        )

    return (
        [columns(at) for at in range(group)] * 2 + [rows(at) for at in range(group)]
    )


def partial_products(block, live, tok, cot, gate_w, up_w, down_w, own_rows):
    row_blocks, capacity = block.shape
    feats = tok.shape[1]
    group = group_of(capacity)
    owners = ROWBLK // own_rows
    rows_spec = pl.BlockSpec((ROWBLK, feats), lambda row, step, block, live: (row, 0))
    flops = 6 * row_blocks * ROWBLK * feats * capacity * BLK
    return pl.pallas_call(
        functools.partial(parts_kernel, group),
        out_shape=jax.ShapeDtypeStruct(
            (row_blocks * owners, 3, own_rows, capacity * BLK), jnp.float32
        ),
        grid_spec=pltpu.PrefetchScalarGridSpec(
            num_scalar_prefetch=2,
            grid=(row_blocks, capacity // group),
            in_specs=[rows_spec, rows_spec] + weight_specs(group, feats),
            out_specs=pl.BlockSpec(
                (owners, 3, own_rows, group * BLK), lambda row, step, block, live: (row, 0, 0, step)
            ),
        ),
        compiler_params=pltpu.CompilerParams(vmem_limit_bytes=VMEM_LIMIT),
        cost_estimate=pl.CostEstimate(
            flops=flops, bytes_accessed=flops // ROWBLK, transcendentals=0
        ),
    )(block, live, tok, cot, *([gate_w] * group + [up_w] * group + [down_w] * group))


def exchange_kernel(
    count, part_ref, all_ref, paired, summed, landed, acts,
    pair_send, pair_recv, sum_send, sum_recv, all_send, all_recv, hand_send, hand_recv, own_sem,
):
    chips = count // 2
    me = lax.axis_index("seq")
    chip, core = me // 2, lax.rem(me, 2)
    sibling = me + 1 - 2 * core
    columns = part_ref.shape[3]
    piece = group_of(columns // BLK) * BLK

    def ahead(shift):
        return lax.rem(chip + shift, chips)

    def behind(shift):
        return lax.rem(chip + chips - shift, chips)

    barrier = pltpu.get_barrier_semaphore()
    pl.semaphore_signal(barrier, inc=1, device_id={"seq": sibling}, device_id_type=MESH)
    for shift in range(1, chips):
        pl.semaphore_signal(
            barrier, inc=1, device_id={"seq": ahead(shift) * 2 + core}, device_id_type=MESH
        )
    pl.semaphore_wait(barrier, chips)

    def pair_copy(shift):
        return pltpu.make_async_remote_copy(
            src_ref=part_ref.at[ahead(shift) * 2 + 1 - core],
            dst_ref=paired.at[shift],
            send_sem=pair_send.at[shift],
            recv_sem=pair_recv.at[shift],
            device_id={"seq": sibling},
            device_id_type=MESH,
        )

    def sum_copy(shift):
        return pltpu.make_async_remote_copy(
            src_ref=summed.at[shift],
            dst_ref=landed.at[shift],
            send_sem=sum_send.at[shift],
            recv_sem=sum_recv.at[shift],
            device_id={"seq": ahead(shift) * 2 + core},
            device_id_type=MESH,
        )

    def all_copy(shift, owner):
        return pltpu.make_async_remote_copy(
            src_ref=acts,
            dst_ref=all_ref.at[owner],
            send_sem=all_send.at[shift],
            recv_sem=all_recv.at[shift],
            device_id={"seq": ahead(shift) * 2 + core},
            device_id_type=MESH,
        )

    def hand_copy(shift, owner):
        return pltpu.make_async_remote_copy(
            src_ref=all_ref.at[owner],
            dst_ref=all_ref.at[owner],
            send_sem=hand_send.at[shift],
            recv_sem=hand_recv.at[shift],
            device_id={"seq": sibling},
            device_id_type=MESH,
        )

    for shift in list(range(1, chips)) + [0]:
        pair_copy(shift).start()

    def send_sum(shift, carry):
        pair_copy(shift).wait_recv()
        mine = ahead(shift) * 2 + core
        for which in range(3):
            for start in range(0, columns, piece):
                cut = slice(start, start + piece)
                summed[shift, which, :, cut] = (
                    part_ref[mine, which, :, cut] + paired[shift, which, :, cut]
                ).astype(jnp.bfloat16)
        sum_copy(shift).start()
        return carry

    lax.fori_loop(1, chips, send_sum, 0)
    pair_copy(0).wait_recv()

    def arrived(shift, carry):
        sum_copy(shift).wait_recv()
        return carry

    lax.fori_loop(1, chips, arrived, 0)

    def act(step, carry):
        cut = pl.ds(pl.multiple_of(step * piece, BLK), piece)

        def total(which):
            value = part_ref[me, which, :, cut] + paired[0, which, :, cut]
            for shift in range(1, chips):
                value = value + landed[shift, which, :, cut].astype(jnp.float32)
            return value

        gate, up, grad = total(0), total(1), total(2)
        sig = jax.nn.sigmoid(gate)
        acts[0, :, cut] = (gate * sig * up).astype(jnp.bfloat16)
        acts[1, :, cut] = (grad * up * sig * (1.0 + gate * (1.0 - sig))).astype(jnp.bfloat16)
        acts[2, :, cut] = (grad * gate * sig).astype(jnp.bfloat16)
        return carry

    lax.fori_loop(0, columns // piece, act, 0)

    for shift in range(1, chips):
        all_copy(shift, me).start()
    own = pltpu.make_async_copy(acts, all_ref.at[me], own_sem)
    own.start()
    first = pltpu.make_async_remote_copy(
        src_ref=acts,
        dst_ref=all_ref.at[me],
        send_sem=hand_send.at[0],
        recv_sem=hand_recv.at[0],
        device_id={"seq": sibling},
        device_id_type=MESH,
    )
    first.start()

    def hand(shift, carry):
        owner = behind(shift) * 2 + core
        all_copy(shift, owner).wait_recv()
        hand_copy(shift, owner).start()
        return carry

    lax.fori_loop(1, chips, hand, 0)
    own.wait()
    first.wait_send()

    def finish(shift, carry):
        hand_copy(shift, behind(shift) * 2 + 1 - core).wait_recv()
        pair_copy(shift).wait_send()
        return carry

    lax.fori_loop(0, chips, finish, 0)

    def sent(shift, carry):
        sum_copy(shift).wait_send()
        all_copy(shift, me).wait_send()
        hand_copy(shift, behind(shift) * 2 + core).wait_send()
        return carry

    lax.fori_loop(1, chips, sent, 0)


def exchange(parts):
    count = lax.axis_size("seq")
    chips = count // 2
    chunk = parts.shape[1:]
    sems = [pltpu.SemaphoreType.DMA((chips,))] * 8
    return pl.pallas_call(
        functools.partial(exchange_kernel, count),
        out_shape=jax.ShapeDtypeStruct(parts.shape, jnp.bfloat16),
        in_specs=[pl.BlockSpec(memory_space=pltpu.VMEM)],
        out_specs=pl.BlockSpec(memory_space=pl.ANY),
        scratch_shapes=[
            pltpu.VMEM((chips,) + chunk, jnp.float32),
            pltpu.VMEM((chips,) + chunk, jnp.bfloat16),
            pltpu.VMEM((chips,) + chunk, jnp.bfloat16),
            pltpu.VMEM(chunk, jnp.bfloat16),
        ]
        + sems
        + [pltpu.SemaphoreType.DMA],
        compiler_params=pltpu.CompilerParams(
            collective_id=1, has_side_effects=True, vmem_limit_bytes=VMEM_LIMIT
        ),
    )(parts)


def rows_out_kernel(group, block_ref, live_ref, act_ref, *refs):
    gates, ups, downs = refs[:group], refs[group : 2 * group], refs[2 * group : 3 * group]
    out_ref = refs[3 * group]
    step = pl.program_id(1)

    @pl.when(step == 0)
    def _():
        out_ref[...] = jnp.zeros_like(out_ref)

    out = jnp.zeros(out_ref.shape[2:], jnp.float32)
    grad = jnp.zeros(out_ref.shape[2:], jnp.float32)
    across = (((1,), (1,)), ((), ()))
    for at in range(group):
        columns = slice(at * BLK, (at + 1) * BLK)
        hid, dgate, dup = (act_ref[:, which, :, columns].reshape(ROWBLK, BLK) for which in range(3))
        out += jnp.dot(hid, downs[at][...], preferred_element_type=jnp.float32)
        grad += lax.dot_general(dgate, gates[at][...], across, preferred_element_type=jnp.float32)
        grad += lax.dot_general(dup, ups[at][...], across, preferred_element_type=jnp.float32)
    out_ref[0, 0] += out
    out_ref[0, 1] += grad


def rows_out(block, live, acts, gate_w, up_w, down_w):
    row_blocks, capacity = block.shape
    own_rows = acts.shape[2]
    feats = gate_w.shape[0]
    group = group_of(capacity)
    owners = ROWBLK // own_rows
    flops = 6 * row_blocks * ROWBLK * feats * capacity * BLK
    return pl.pallas_call(
        functools.partial(rows_out_kernel, group),
        out_shape=jax.ShapeDtypeStruct((row_blocks, 2, ROWBLK, feats), jnp.float32),
        grid_spec=pltpu.PrefetchScalarGridSpec(
            num_scalar_prefetch=2,
            grid=(row_blocks, capacity // group),
            in_specs=[
                pl.BlockSpec(
                    (owners, 3, own_rows, group * BLK),
                    lambda row, step, block, live: (row, 0, 0, step),
                )
            ]
            + weight_specs(group, feats),
            out_specs=pl.BlockSpec(
                (1, 2, ROWBLK, feats), lambda row, step, block, live: (row, 0, 0, 0)
            ),
        ),
        compiler_params=pltpu.CompilerParams(vmem_limit_bytes=VMEM_LIMIT),
        cost_estimate=pl.CostEstimate(
            flops=flops, bytes_accessed=flops // ROWBLK, transcendentals=0
        ),
    )(block, live, acts, *([gate_w] * group + [up_w] * group + [down_w] * group))


def weights_out_kernel(
    group, scale, slot_ref, mask_ref, tok_ref, cot_ref, act_ref, gate_ref, up_ref, down_ref,
    flipped, dense,
):
    step = pl.program_id(0)
    row_blocks = mask_ref.shape[0]
    owners = ROWBLK // act_ref.shape[2]

    @pl.when(step == 0)
    def _():
        flipped[...] = tok_ref[...].T

    for at in range(group):
        for row in range(row_blocks):
            kept = mask_ref[row, step * group + at] == 1
            slot = pl.ds(pl.multiple_of(slot_ref[row, step * group + at] * BLK, BLK), BLK)
            for which in range(3):
                value = act_ref[row * owners : (row + 1) * owners, which, :, slot]
                value = jnp.where(kept, value, jnp.zeros_like(value))
                dense[which, row * ROWBLK : (row + 1) * ROWBLK, at * BLK : (at + 1) * BLK] = (
                    value.reshape(ROWBLK, BLK)
                )
    tok = flipped[...]
    gate_ref[...] = jnp.dot(tok, dense[1], preferred_element_type=jnp.float32) * scale
    up_ref[...] = jnp.dot(tok, dense[2], preferred_element_type=jnp.float32) * scale
    down_ref[...] = (
        lax.dot_general(
            dense[0], cot_ref[...], (((0,), (0,)), ((), ())), preferred_element_type=jnp.float32
        )
        * scale
    )


def weights_out(slots, masks, tok, cot, acts):
    row_blocks, blocks = masks.shape
    rows, feats = tok.shape
    group = group_of(blocks)
    whole = pl.BlockSpec((rows, feats), lambda step, slot, mask: (0, 0))
    wide = pl.BlockSpec((feats, group * BLK), lambda step, slot, mask: (0, step))
    hidden = blocks * BLK
    return pl.pallas_call(
        functools.partial(weights_out_kernel, group, 1.0 / math.sqrt(rows)),
        out_shape=(
            jax.ShapeDtypeStruct((feats, hidden), jnp.float32),
            jax.ShapeDtypeStruct((feats, hidden), jnp.float32),
            jax.ShapeDtypeStruct((hidden, feats), jnp.float32),
        ),
        grid_spec=pltpu.PrefetchScalarGridSpec(
            num_scalar_prefetch=2,
            grid=(blocks // group,),
            in_specs=[
                whole,
                whole,
                pl.BlockSpec(acts.shape, lambda step, slot, mask: (0, 0, 0, 0)),
            ],
            out_specs=(
                wide,
                wide,
                pl.BlockSpec((group * BLK, feats), lambda step, slot, mask: (step, 0)),
            ),
            scratch_shapes=[
                pltpu.VMEM((feats, rows), jnp.bfloat16),
                pltpu.VMEM((3, rows, group * BLK), jnp.bfloat16),
            ],
        ),
        compiler_params=pltpu.CompilerParams(vmem_limit_bytes=VMEM_LIMIT),
        cost_estimate=pl.CostEstimate(
            flops=6 * rows * feats * hidden, bytes_accessed=12 * feats * hidden, transcendentals=0
        ),
    )(slots, masks, tok, cot, acts)


def shards(tokens, gate_weight, up_weight, down_weight, masks, cotangent):
    seq_count = lax.axis_size("seq")
    tp_count = lax.axis_size("tp")
    rank = lax.axis_index("tp")
    rows, feats = tokens.shape
    total_rows = rows * tp_count
    kept_total = masks.shape[1] * tp_count // KEEP_PART
    capacity = min(2 * kept_total // tp_count, masks.shape[1])
    tok, cot = (value.reshape(total_rows, feats) for value in gather_rows(tokens, cotangent))
    block, live, slots = slot_tables(masks, capacity)
    parts = partial_products(
        block, live, tok, cot, gate_weight, up_weight, down_weight, total_rows // seq_count
    )
    acts = exchange(parts)
    row_parts = rows_out(block, live, acts, gate_weight, up_weight, down_weight)
    row_parts = jnp.swapaxes(row_parts.reshape(tp_count, rows // ROWBLK, 2, ROWBLK, feats), 1, 2)
    moved = []
    for shift in range(1, tp_count):
        piece = lax.dynamic_index_in_dim(
            row_parts, lax.rem(rank + shift, tp_count), 0, keepdims=False
        ).astype(jnp.bfloat16)
        pairs = [(src, (src + shift) % tp_count) for src in range(tp_count)]
        moved.append(lax.ppermute(piece, "tp", pairs))
    grad_gate, grad_up, grad_down = weights_out(slots, masks, tok, cot, acts)
    mine = lax.dynamic_index_in_dim(row_parts, rank, 0, keepdims=False)
    for piece in moved:
        mine = mine + piece.astype(jnp.float32)
    mine = mine.reshape(2, rows, feats).astype(jnp.bfloat16)
    return (mine[0], mine[1], grad_gate, grad_up, grad_down)


def solution(mesh):
    placed = (
        P("tp", "seq"),
        P("seq", "tp"),
        P("seq", "tp"),
        P("tp", "seq"),
        P(None, "tp"),
        P("tp", "seq"),
    )
    return jax.shard_map(
        shards,
        mesh=mesh,
        in_specs=placed,
        out_specs=(P("tp", "seq"), P("tp", "seq"), P("seq", "tp"), P("seq", "tp"), P("tp", "seq")),
        check_vma=False,
    )
```

time: 582 us -> 212 us (0.36)
  the two profiles are of different devices: /device:TPU:0 before, /device:TPU:27 now
where the time goes in v1:
time: 212 us; the launch traced here: 211 us
  Pallas kernels  208 us (98%)
    pallas_call x1, Pallas kernels, exchange(): pl.pallas_call(functools.partial(exchange_kernel, count), out_shape=jax.S...  145 us
    pallas_call x1, Pallas kernels, weights_out(): pl.pallas_call(functools.partial(weights_out_kernel, group, 1.0 / math.sq...  18.5 us
    pallas_call x1, Pallas kernels, partial_products(): pl.pallas_call(functools.partial(parts_kernel, group), out_shape=jax.Shap...  16.4 us
    pallas_call x1, Pallas kernels, rows_out(): pl.pallas_call(functools.partial(rows_out_kernel, group), out_shape=jax.S...  15.9 us
    pallas_call x1, Pallas kernels, gather_rows(): pl.pallas_call(functools.partial(rows_kernel, count), out_shape=(jax.Shap...  10.4 us
  transfers between devices with their start and end apart: 1, of which 0 were waited for; matrix products, arithmetic and copies ran while one was open for 0% of the time, Pallas kernels for 9%

profile of v1, /device:TPU:27, one launch (start us, length us, event | category | flops | bytes accessed | tf_op | source)
XLA Modules:
  0.0 211.1 jit_solution(5983348028503759811)
XLA Ops:
  0.6 2.6 %shard_map.101 = (s32[2,28]{1,0:T(2,128)}, s32[2,28]{1,0:T(2,128)}, s32[2,56]{1,0:T(2,128)}) custom-call(s32[2,56]{1,0:T(2,128)} %mask_ref.3), custom_call_target="tpu_custom_call" | custom-call | tf_op jit(solution)/shard_map/pallas_call | solution.py:51
  3.3 10.4 %shard_map.102 = (bf16[2,128,512]{2,1,0:T(8,128)(2,1)}, bf16[2,128,512]{2,1,0:T(8,128)(2,1)}) custom-call(bf16[128,512]{1,0:T(8,128)(2,1)} %tok_ref.1, bf16[128,512]{1,0:T(8,128)(2,1)} %cot_ref.1), custom_call_target="tpu_custom_call" | custom-call | tf_op jit(solution)/shard_map/pallas_call | solution.py:95
  13.7 16.4 %shard_map.103.part_ref = f32[16,3,16,3584]{3,2,1,0:T(8,128)} custom-call(s32[2,28]{1,0:T(2,128)} %get-tuple-element.13.block_ref, s32[2,28]{1,0:T(2,128)} %get-tuple-element.14.live_ref, bf16[256,512]{1,0:T(8,128)(2,1)} %bitcast.12, bf16[256,512]{1,0:T(8,128)(2,1)} %bitcast.14, bf16[512,7168]{1,0:T(8,128)(2,1)} %refs_6_.3, bf16[512,7168]{1,0:T(8,128)(2,1)} %refs_6_.3, ...), custom_call_target="tpu_custom_call" | custom-call | flops 2818572288 | bytes 22020096 | tf_op jit(solution)/shard_map/pallas_call | solution.py:152
  30.1 144.6 %shard_map.104.act_ref = bf16[16,3,16,3584]{3,2,1,0:T(8,128)(2,1)} custom-call(f32[16,3,16,3584]{3,2,1,0:T(8,128)} %shard_map.103.part_ref), custom_call_target="tpu_custom_call" | custom-call | tf_op jit(solution)/shard_map/pallas_call | solution.py:324
  174.7 15.9 %shard_map.105 = f32[2,2,128,512]{3,2,1,0:T(8,128)} custom-call(s32[2,28]{1,0:T(2,128)} %get-tuple-element.13.block_ref, s32[2,28]{1,0:T(2,128)} %get-tuple-element.14.live_ref, bf16[16,3,16,3584]{3,2,1,0:T(8,128)(2,1)} %shard_map.104.act_ref, bf16[512,7168]{1,0:T(8,128)(2,1)} %refs_6_.3, bf16[512,7168]{1,0:T(8,128)(2,1)} %refs_6_.3, ...), custom_call_target="tpu_custom_call" | custom-call | flops 2818572288 | bytes 22020096 | tf_op jit(solution)/shard_map/pallas_call | solution.py:372
  190.6 0.0 copy-start
  190.6 1.2 fusion.1
  191.8 0.1 collective-permute-start
  191.9 18.5 %shard_map.106 = (f32[512,7168]{1,0:T(8,128)}, f32[512,7168]{1,0:T(8,128)}, f32[7168,512]{1,0:T(8,128)}) custom-call(s32[2,56]{1,0:T(2,128)} %get-tuple-element.17.slot_ref, s32[2,56]{1,0:T(2,128)} %mask_ref.3, bf16[256,512]{1,0:T(8,128)(2,1)} %bitcast.13, bf16[256,512]{1,0:T(8,128)(2,1)} %bitcast.15, bf16[16,3,16,3584]{3,2,1,0:T(8,128)(2,1)} %shard_map.104.act_ref), custom_call_target="tpu_custom_call" | custom-call | flops 5637144576 | bytes 44040192 | tf_op jit(solution)/shard_map/pallas_call | solution.py:436
  210.3 0.0 collective-permute-done
  210.3 0.0 copy-done
  210.3 0.1 fusion
  210.4 0.7 slice_bitcast_fusion
Async XLA Ops:
  190.6 19.7 %copy-start = (f32[2,2,128,512]{3,2,1,0:T(8,128)S(1)}, f32[2,2,128,512]{3,2,1,0:T(8,128)}, u32[]{:S(2)}) copy-start(f32[2,2,128,512]{3,2,1,0:T(8,128)} %shard_map.105) | copy-start | bytes 3145732
  191.8 18.5 %collective-permute-start = (bf16[2,1,128,512]{3,2,0,1:T(8,128)(2,1)S(1)}, bf16[2,1,128,512]{3,2,0,1:T(8,128)(2,1)S(1)}, u32[]{:S(2)}, u32[]{:S(2)}) collective-permute-start(bf16[2,1,128,512]{3,2,0,1:T(8,128)(2,1)S(1)} %fusion.1), channel_id=1, source_target_pairs={{0,1},{1,0},{2,3},{3,2},{4,5},{5,4},{6,7},{7,6},{8,9},{9,8},{10,11... | collective-permute-start | bytes 786440 | tf_op jit(solution)/shard_map/ppermute | solution.py:490

commit v2 on v1

--- a/solution.py
+++ b/solution.py
@@ -171,20 +171,21 @@
 
 def exchange_kernel(
     count, part_ref, all_ref, paired, summed, landed, acts,
-    pair_send, pair_recv, sum_send, sum_recv, all_send, all_recv, hand_send, hand_recv, own_sem,
+    pair_send, pair_recv, sum_send, sum_recv, side_send, up_send, down_send, all_recv,
+    hand_send, hand_recv, own_sem,
 ):
     chips = count // 2
     me = lax.axis_index("seq")
     chip, core = me // 2, lax.rem(me, 2)
     sibling = me + 1 - 2 * core
+    tall = 4 if chips % 4 == 0 else chips
+    wide = chips // tall
+    along, across = chip // wide, lax.rem(chip, wide)
     columns = part_ref.shape[3]
     piece = group_of(columns // BLK) * BLK
 
     def ahead(shift):
         return lax.rem(chip + shift, chips)
-
-    def behind(shift):
-        return lax.rem(chip + chips - shift, chips)
 
     barrier = pltpu.get_barrier_semaphore()
     pl.semaphore_signal(barrier, inc=1, device_id={"seq": sibling}, device_id_type=MESH)
@@ -214,22 +215,24 @@
             device_id_type=MESH,
         )
 
-    def all_copy(shift, owner):
+    def route(owner, dest, send, src=None):
+        slot = all_ref.at[owner * 2 + core]
         return pltpu.make_async_remote_copy(
-            src_ref=acts,
-            dst_ref=all_ref.at[owner],
-            send_sem=all_send.at[shift],
-            recv_sem=all_recv.at[shift],
-            device_id={"seq": ahead(shift) * 2 + core},
+            src_ref=slot if src is None else src,
+            dst_ref=slot,
+            send_sem=send.at[owner],
+            recv_sem=all_recv.at[owner],
+            device_id={"seq": dest * 2 + core},
             device_id_type=MESH,
         )
 
-    def hand_copy(shift, owner):
+    def hand_copy(owner, side, src=None):
+        slot = all_ref.at[owner * 2 + side]
         return pltpu.make_async_remote_copy(
-            src_ref=all_ref.at[owner],
-            dst_ref=all_ref.at[owner],
-            send_sem=hand_send.at[shift],
-            recv_sem=hand_recv.at[shift],
+            src_ref=slot if src is None else src,
+            dst_ref=slot,
+            send_sem=hand_send.at[owner],
+            recv_sem=hand_recv.at[owner],
             device_id={"seq": sibling},
             device_id_type=MESH,
         )
@@ -276,41 +279,86 @@
 
     lax.fori_loop(0, columns // piece, act, 0)
 
-    for shift in range(1, chips):
-        all_copy(shift, me).start()
     own = pltpu.make_async_copy(acts, all_ref.at[me], own_sem)
     own.start()
-    first = pltpu.make_async_remote_copy(
-        src_ref=acts,
-        dst_ref=all_ref.at[me],
-        send_sem=hand_send.at[0],
-        recv_sem=hand_recv.at[0],
-        device_id={"seq": sibling},
-        device_id_type=MESH,
-    )
-    first.start()
-
-    def hand(shift, carry):
-        owner = behind(shift) * 2 + core
-        all_copy(shift, owner).wait_recv()
-        hand_copy(shift, owner).start()
-        return carry
-
-    lax.fori_loop(1, chips, hand, 0)
+
+    def aside(step):
+        return lax.rem(across + step, wide)
+
+    def pass_on(owner, up, down, src=None):
+        @pl.when(jnp.logical_and(up, along < tall - 1))
+        def _():
+            route(owner, chip + wide, up_send, src).start()
+
+        @pl.when(jnp.logical_and(down, along > 0))
+        def _():
+            route(owner, chip - wide, down_send, src).start()
+
+        hand_copy(owner, core, src).start()
+
+    def take(owner):
+        route(owner, chip, up_send).wait_recv()
+
+    yes, no = jnp.bool_(True), jnp.bool_(False)
+    for step in range(1, wide):
+        pltpu.make_async_remote_copy(
+            src_ref=acts,
+            dst_ref=all_ref.at[me],
+            send_sem=side_send.at[step],
+            recv_sem=all_recv.at[chip],
+            device_id={"seq": (along * wide + aside(step)) * 2 + core},
+            device_id_type=MESH,
+        ).start()
+    pass_on(chip, yes, yes, acts)
+    for step in range(1, wide):
+        owner = along * wide + aside(step)
+        take(owner)
+        pass_on(owner, yes, yes)
+    for far in range(1, tall):
+        for step in range(wide):
+
+            @pl.when(along >= far)
+            def _():
+                owner = (along - far) * wide + aside(step)
+                take(owner)
+                pass_on(owner, yes, no)
+
+            @pl.when(along + far < tall)
+            def _():
+                owner = (along + far) * wide + aside(step)
+                take(owner)
+                pass_on(owner, no, yes)
+
     own.wait()
-    first.wait_send()
-
-    def finish(shift, carry):
-        hand_copy(shift, behind(shift) * 2 + 1 - core).wait_recv()
-        pair_copy(shift).wait_send()
+    for step in range(1, wide):
+        pltpu.make_async_remote_copy(
+            src_ref=acts,
+            dst_ref=all_ref.at[me],
+            send_sem=side_send.at[step],
+            recv_sem=all_recv.at[chip],
+            device_id={"seq": (along * wide + aside(step)) * 2 + core},
+            device_id_type=MESH,
+        ).wait_send()
+
+    def finish(owner, carry):
+        hand_copy(owner, 1 - core).wait_recv()
+        hand_copy(owner, core).wait_send()
+        pair_copy(owner).wait_send()
+
+        @pl.when(jnp.logical_and(owner // wide <= along, along < tall - 1))
+        def _():
+            route(owner, chip + wide, up_send).wait_send()
+
+        @pl.when(jnp.logical_and(owner // wide >= along, along > 0))
+        def _():
+            route(owner, chip - wide, down_send).wait_send()
+
         return carry
 
     lax.fori_loop(0, chips, finish, 0)
 
     def sent(shift, carry):
         sum_copy(shift).wait_send()
-        all_copy(shift, me).wait_send()
-        hand_copy(shift, behind(shift) * 2 + core).wait_send()
         return carry
 
     lax.fori_loop(1, chips, sent, 0)
@@ -320,7 +368,7 @@
     count = lax.axis_size("seq")
     chips = count // 2
     chunk = parts.shape[1:]
-    sems = [pltpu.SemaphoreType.DMA((chips,))] * 8
+    sems = [pltpu.SemaphoreType.DMA((chips,))] * 10
     return pl.pallas_call(
         functools.partial(exchange_kernel, count),
         out_shape=jax.ShapeDtypeStruct(parts.shape, jnp.bfloat16),

time: 212 us -> 192 us (0.906)
  the two profiles are of different devices: /device:TPU:27 before, /device:TPU:0 now
where the time goes in v2:
time: 192 us; the launch traced here: 191 us
  Pallas kernels  188 us (98%)
    pallas_call x1, Pallas kernels, exchange(): pl.pallas_call(functools.partial(exchange_kernel, count), out_shape=jax.S...  123 us
    pallas_call x1, Pallas kernels, weights_out(): pl.pallas_call(functools.partial(weights_out_kernel, group, 1.0 / math.sq...  18.5 us
    pallas_call x1, Pallas kernels, partial_products(): pl.pallas_call(functools.partial(parts_kernel, group), out_shape=jax.Shap...  16.4 us
    pallas_call x1, Pallas kernels, rows_out(): pl.pallas_call(functools.partial(rows_out_kernel, group), out_shape=jax.S...  15.8 us
    pallas_call x1, Pallas kernels, gather_rows(): pl.pallas_call(functools.partial(rows_kernel, count), out_shape=(jax.Shap...  12.2 us
  transfers between devices with their start and end apart: 1, of which 0 were waited for; matrix products, arithmetic and copies ran while one was open for 0% of the time, Pallas kernels for 10%

profile of v2, /device:TPU:0, one launch (start us, length us, event | category | flops | bytes accessed | tf_op | source)
XLA Modules:
  0.0 190.8 jit_solution(8221469610220870048)
XLA Ops:
  0.6 2.6 %shard_map.101 = (s32[2,28]{1,0:T(2,128)}, s32[2,28]{1,0:T(2,128)}, s32[2,56]{1,0:T(2,128)}) custom-call(s32[2,56]{1,0:T(2,128)} %mask_ref.3), custom_call_target="tpu_custom_call" | custom-call | tf_op jit(solution)/shard_map/pallas_call | solution.py:51
  3.3 12.2 %shard_map.102 = (bf16[2,128,512]{2,1,0:T(8,128)(2,1)}, bf16[2,128,512]{2,1,0:T(8,128)(2,1)}) custom-call(bf16[128,512]{1,0:T(8,128)(2,1)} %tok_ref.1, bf16[128,512]{1,0:T(8,128)(2,1)} %cot_ref.1), custom_call_target="tpu_custom_call" | custom-call | tf_op jit(solution)/shard_map/pallas_call | solution.py:95
  15.5 16.4 %shard_map.103.part_ref = f32[16,3,16,3584]{3,2,1,0:T(8,128)} custom-call(s32[2,28]{1,0:T(2,128)} %get-tuple-element.13.block_ref, s32[2,28]{1,0:T(2,128)} %get-tuple-element.14.live_ref, bf16[256,512]{1,0:T(8,128)(2,1)} %bitcast.12, bf16[256,512]{1,0:T(8,128)(2,1)} %bitcast.14, bf16[512,7168]{1,0:T(8,128)(2,1)} %refs_6_.3, bf16[512,7168]{1,0:T(8,128)(2,1)} %refs_6_.3, ...), custom_call_target="tpu_custom_call" | custom-call | flops 2818572288 | bytes 22020096 | tf_op jit(solution)/shard_map/pallas_call | solution.py:152
  31.8 122.6 %shard_map.104.act_ref = bf16[16,3,16,3584]{3,2,1,0:T(8,128)(2,1)} custom-call(f32[16,3,16,3584]{3,2,1,0:T(8,128)} %shard_map.103.part_ref), custom_call_target="tpu_custom_call" | custom-call | tf_op jit(solution)/shard_map/pallas_call | solution.py:372
  154.5 15.8 %shard_map.105 = f32[2,2,128,512]{3,2,1,0:T(8,128)} custom-call(s32[2,28]{1,0:T(2,128)} %get-tuple-element.13.block_ref, s32[2,28]{1,0:T(2,128)} %get-tuple-element.14.live_ref, bf16[16,3,16,3584]{3,2,1,0:T(8,128)(2,1)} %shard_map.104.act_ref, bf16[512,7168]{1,0:T(8,128)(2,1)} %refs_6_.3, bf16[512,7168]{1,0:T(8,128)(2,1)} %refs_6_.3, ...), custom_call_target="tpu_custom_call" | custom-call | flops 2818572288 | bytes 22020096 | tf_op jit(solution)/shard_map/pallas_call | solution.py:420
  170.2 0.0 copy-start
  170.3 1.2 fusion.1
  171.4 0.1 collective-permute-start
  171.5 18.5 %shard_map.106 = (f32[512,7168]{1,0:T(8,128)}, f32[512,7168]{1,0:T(8,128)}, f32[7168,512]{1,0:T(8,128)}) custom-call(s32[2,56]{1,0:T(2,128)} %get-tuple-element.17.slot_ref, s32[2,56]{1,0:T(2,128)} %mask_ref.3, bf16[256,512]{1,0:T(8,128)(2,1)} %bitcast.13, bf16[256,512]{1,0:T(8,128)(2,1)} %bitcast.15, bf16[16,3,16,3584]{3,2,1,0:T(8,128)(2,1)} %shard_map.104.act_ref), custom_call_target="tpu_custom_call" | custom-call | flops 5637144576 | bytes 44040192 | tf_op jit(solution)/shard_map/pallas_call | solution.py:484
  190.0 0.0 collective-permute-done
  190.0 0.0 copy-done
  190.0 0.1 fusion
  190.1 0.7 slice_bitcast_fusion
Async XLA Ops:
  170.2 19.7 %copy-start = (f32[2,2,128,512]{3,2,1,0:T(8,128)S(1)}, f32[2,2,128,512]{3,2,1,0:T(8,128)}, u32[]{:S(2)}) copy-start(f32[2,2,128,512]{3,2,1,0:T(8,128)} %shard_map.105) | copy-start | bytes 3145732
  171.4 18.5 %collective-permute-start = (bf16[2,1,128,512]{3,2,0,1:T(8,128)(2,1)S(1)}, bf16[2,1,128,512]{3,2,0,1:T(8,128)(2,1)S(1)}, u32[]{:S(2)}, u32[]{:S(2)}) collective-permute-start(bf16[2,1,128,512]{3,2,0,1:T(8,128)(2,1)S(1)} %fusion.1), channel_id=1, source_target_pairs={{0,1},{1,0},{2,3},{3,2},{4,5},{5,4},{6,7},{7,6},{8,9},{9,8},{10,11... | collective-permute-start | bytes 786440 | tf_op jit(solution)/shard_map/ppermute | solution.py:538

commit v3 on v1

--- a/solution.py
+++ b/solution.py
@@ -171,20 +171,23 @@
 
 def exchange_kernel(
     count, part_ref, all_ref, paired, summed, landed, acts,
-    pair_send, pair_recv, sum_send, sum_recv, all_send, all_recv, hand_send, hand_recv, own_sem,
+    pair_send, pair_recv, sum_send, sum_recv, side_send, up_send, down_send, all_recv,
+    hand_send, hand_recv, own_sem,
 ):
     chips = count // 2
     me = lax.axis_index("seq")
     chip, core = me // 2, lax.rem(me, 2)
     sibling = me + 1 - 2 * core
+    tall = 4 if chips % 4 == 0 else chips
+    wide = chips // tall
+    along, across = chip // wide, lax.rem(chip, wide)
     columns = part_ref.shape[3]
     piece = group_of(columns // BLK) * BLK
+    halves = 2 if columns // piece % 2 == 0 else 1
+    width = columns // halves
 
     def ahead(shift):
         return lax.rem(chip + shift, chips)
-
-    def behind(shift):
-        return lax.rem(chip + chips - shift, chips)
 
     barrier = pltpu.get_barrier_semaphore()
     pl.semaphore_signal(barrier, inc=1, device_id={"seq": sibling}, device_id_type=MESH)
@@ -204,32 +207,37 @@
             device_id_type=MESH,
         )
 
-    def sum_copy(shift):
+    def part_of(half):
+        return slice(half * width, (half + 1) * width)
+
+    def sum_copy(half, shift):
         return pltpu.make_async_remote_copy(
-            src_ref=summed.at[shift],
-            dst_ref=landed.at[shift],
-            send_sem=sum_send.at[shift],
-            recv_sem=sum_recv.at[shift],
+            src_ref=summed.at[shift, :, :, part_of(half)],
+            dst_ref=landed.at[shift, :, :, part_of(half)],
+            send_sem=sum_send.at[half, shift],
+            recv_sem=sum_recv.at[half, shift],
             device_id={"seq": ahead(shift) * 2 + core},
             device_id_type=MESH,
         )
 
-    def all_copy(shift, owner):
+    def route(half, owner, dest, send, src=None):
+        slot = all_ref.at[owner * 2 + core, :, :, part_of(half)]
         return pltpu.make_async_remote_copy(
-            src_ref=acts,
-            dst_ref=all_ref.at[owner],
-            send_sem=all_send.at[shift],
-            recv_sem=all_recv.at[shift],
-            device_id={"seq": ahead(shift) * 2 + core},
+            src_ref=slot if src is None else src,
+            dst_ref=slot,
+            send_sem=send.at[half, owner],
+            recv_sem=all_recv.at[half, owner],
+            device_id={"seq": dest * 2 + core},
             device_id_type=MESH,
         )
 
-    def hand_copy(shift, owner):
+    def hand_copy(half, owner, side, src=None):
+        slot = all_ref.at[owner * 2 + side, :, :, part_of(half)]
         return pltpu.make_async_remote_copy(
-            src_ref=all_ref.at[owner],
-            dst_ref=all_ref.at[owner],
-            send_sem=hand_send.at[shift],
-            recv_sem=hand_recv.at[shift],
+            src_ref=slot if src is None else src,
+            dst_ref=slot,
+            send_sem=hand_send.at[half, owner],
+            recv_sem=hand_recv.at[half, owner],
             device_id={"seq": sibling},
             device_id_type=MESH,
         )
@@ -237,26 +245,26 @@
     for shift in list(range(1, chips)) + [0]:
         pair_copy(shift).start()
 
-    def send_sum(shift, carry):
-        pair_copy(shift).wait_recv()
+    def send_sum(half, shift, carry):
+        if half == 0:
+            pair_copy(shift).wait_recv()
         mine = ahead(shift) * 2 + core
         for which in range(3):
-            for start in range(0, columns, piece):
+            for start in range(half * width, (half + 1) * width, piece):
                 cut = slice(start, start + piece)
                 summed[shift, which, :, cut] = (
                     part_ref[mine, which, :, cut] + paired[shift, which, :, cut]
                 ).astype(jnp.bfloat16)
-        sum_copy(shift).start()
+        sum_copy(half, shift).start()
         return carry
 
-    lax.fori_loop(1, chips, send_sum, 0)
+    for half in range(halves):
+        lax.fori_loop(1, chips, functools.partial(send_sum, half), 0)
     pair_copy(0).wait_recv()
 
-    def arrived(shift, carry):
-        sum_copy(shift).wait_recv()
+    def arrived(half, shift, carry):
+        sum_copy(half, shift).wait_recv()
         return carry
-
-    lax.fori_loop(1, chips, arrived, 0)
 
     def act(step, carry):
         cut = pl.ds(pl.multiple_of(step * piece, BLK), piece)
@@ -274,53 +282,104 @@
         acts[2, :, cut] = (grad * gate * sig).astype(jnp.bfloat16)
         return carry
 
-    lax.fori_loop(0, columns // piece, act, 0)
-
-    for shift in range(1, chips):
-        all_copy(shift, me).start()
-    own = pltpu.make_async_copy(acts, all_ref.at[me], own_sem)
-    own.start()
-    first = pltpu.make_async_remote_copy(
-        src_ref=acts,
-        dst_ref=all_ref.at[me],
-        send_sem=hand_send.at[0],
-        recv_sem=hand_recv.at[0],
-        device_id={"seq": sibling},
-        device_id_type=MESH,
-    )
-    first.start()
-
-    def hand(shift, carry):
-        owner = behind(shift) * 2 + core
-        all_copy(shift, owner).wait_recv()
-        hand_copy(shift, owner).start()
-        return carry
-
-    lax.fori_loop(1, chips, hand, 0)
-    own.wait()
-    first.wait_send()
-
-    def finish(shift, carry):
-        hand_copy(shift, behind(shift) * 2 + 1 - core).wait_recv()
-        pair_copy(shift).wait_send()
-        return carry
-
-    lax.fori_loop(0, chips, finish, 0)
-
-    def sent(shift, carry):
-        sum_copy(shift).wait_send()
-        all_copy(shift, me).wait_send()
-        hand_copy(shift, behind(shift) * 2 + core).wait_send()
-        return carry
-
-    lax.fori_loop(1, chips, sent, 0)
+    def aside(step):
+        return lax.rem(across + step, wide)
+
+    def pass_on(half, owner, up, down, src=None):
+        @pl.when(jnp.logical_and(up, along < tall - 1))
+        def _():
+            route(half, owner, chip + wide, up_send, src).start()
+
+        @pl.when(jnp.logical_and(down, along > 0))
+        def _():
+            route(half, owner, chip - wide, down_send, src).start()
+
+        hand_copy(half, owner, core, src).start()
+
+    def take(half, owner):
+        route(half, owner, chip, up_send).wait_recv()
+
+    for half in range(halves):
+        lax.fori_loop(1, chips, functools.partial(arrived, half), 0)
+        steps = width // piece
+        lax.fori_loop(half * steps, (half + 1) * steps, act, 0)
+
+        own = pltpu.make_async_copy(acts.at[:, :, part_of(half)], all_ref.at[me, :, :, part_of(half)], own_sem.at[half])
+        own.start()
+
+        yes, no = jnp.bool_(True), jnp.bool_(False)
+        for step in range(1, wide):
+            pltpu.make_async_remote_copy(
+                src_ref=acts.at[:, :, part_of(half)],
+                dst_ref=all_ref.at[me, :, :, part_of(half)],
+                send_sem=side_send.at[half, step],
+                recv_sem=all_recv.at[half, chip],
+                device_id={"seq": (along * wide + aside(step)) * 2 + core},
+                device_id_type=MESH,
+            ).start()
+        pass_on(half, chip, yes, yes, acts.at[:, :, part_of(half)])
+        for step in range(1, wide):
+            owner = along * wide + aside(step)
+            take(half, owner)
+            pass_on(half, owner, yes, yes)
+        for far in range(1, tall):
+            for step in range(wide):
+
+                @pl.when(along >= far)
+                def _():
+                    owner = (along - far) * wide + aside(step)
+                    take(half, owner)
+                    pass_on(half, owner, yes, no)
+
+                @pl.when(along + far < tall)
+                def _():
+                    owner = (along + far) * wide + aside(step)
+                    take(half, owner)
+                    pass_on(half, owner, no, yes)
+
+    for half in range(halves):
+        pltpu.make_async_copy(acts.at[:, :, part_of(half)], all_ref.at[me, :, :, part_of(half)], own_sem.at[half]).wait()
+        for step in range(1, wide):
+            pltpu.make_async_remote_copy(
+                src_ref=acts.at[:, :, part_of(half)],
+                dst_ref=all_ref.at[me, :, :, part_of(half)],
+                send_sem=side_send.at[half, step],
+                recv_sem=all_recv.at[half, chip],
+                device_id={"seq": (along * wide + aside(step)) * 2 + core},
+                device_id_type=MESH,
+            ).wait_send()
+
+        def finish(owner, carry):
+            hand_copy(half, owner, 1 - core).wait_recv()
+            hand_copy(half, owner, core).wait_send()
+            if half == 0:
+                pair_copy(owner).wait_send()
+
+            @pl.when(jnp.logical_and(owner // wide <= along, along < tall - 1))
+            def _():
+                route(half, owner, chip + wide, up_send).wait_send()
+
+            @pl.when(jnp.logical_and(owner // wide >= along, along > 0))
+            def _():
+                route(half, owner, chip - wide, down_send).wait_send()
+
+            return carry
+
+        lax.fori_loop(0, chips, finish, 0)
+
+        def sent(shift, carry):
+            sum_copy(half, shift).wait_send()
+            return carry
+
+        lax.fori_loop(1, chips, sent, 0)
 
 
 def exchange(parts):
     count = lax.axis_size("seq")
     chips = count // 2
     chunk = parts.shape[1:]
-    sems = [pltpu.SemaphoreType.DMA((chips,))] * 8
+    pair = [pltpu.SemaphoreType.DMA((chips,))] * 2
+    sems = pair + [pltpu.SemaphoreType.DMA((2, chips))] * 8
     return pl.pallas_call(
         functools.partial(exchange_kernel, count),
         out_shape=jax.ShapeDtypeStruct(parts.shape, jnp.bfloat16),
@@ -333,7 +392,7 @@
             pltpu.VMEM(chunk, jnp.bfloat16),
         ]
         + sems
-        + [pltpu.SemaphoreType.DMA],
+        + [pltpu.SemaphoreType.DMA((2,))],
         compiler_params=pltpu.CompilerParams(
             collective_id=1, has_side_effects=True, vmem_limit_bytes=VMEM_LIMIT
         ),

time: 212 us -> 186 us (0.88)
  the two profiles are of different devices: /device:TPU:27 before, /device:TPU:0 now
where the time goes in v3:
time: 186 us
  Pallas kernels  180 us (97%)
  starting transfers between devices  2.99 us (2%)
  local copies, waits for them, and re-layouts  1.88 us (1%)
    pallas_call x1, Pallas kernels, exchange(): pl.pallas_call(functools.partial(exchange_kernel, count), out_shape=jax.S...  117 us
    pallas_call x1, Pallas kernels, weights_out(): pl.pallas_call(functools.partial(weights_out_kernel, group, 1.0 / math.sq...  18.5 us
    pallas_call x1, Pallas kernels, rows_out(): pl.pallas_call(functools.partial(rows_out_kernel, group), out_shape=jax.S...  14.9 us
    pallas_call x1, Pallas kernels, partial_products(): pl.pallas_call(functools.partial(parts_kernel, group), out_shape=jax.Shap...  14.8 us
    pallas_call x1, Pallas kernels, gather_rows(): pl.pallas_call(functools.partial(rows_kernel, count), out_shape=(jax.Shap...  12.2 us
  transfers between devices with their start and end apart: 1, of which 0 were waited for; matrix products, arithmetic and copies ran while one was open for 0% of the time, Pallas kernels for 10%

profile of v3, /device:TPU:0, one launch (start us, length us, event | category | flops | bytes accessed | tf_op | source)
XLA Modules:
  0.0 185.7 jit_solution(9343801627868962913)
XLA Ops:
  0.6 2.6 %shard_map.101 = (s32[2,28]{1,0:T(2,128)}, s32[2,28]{1,0:T(2,128)}, s32[2,56]{1,0:T(2,128)}) custom-call(s32[2,56]{1,0:T(2,128)} %mask_ref.3), custom_call_target="tpu_custom_call" | custom-call | tf_op jit(solution)/shard_map/pallas_call | solution.py:51
  3.3 12.2 %shard_map.102 = (bf16[2,128,512]{2,1,0:T(8,128)(2,1)}, bf16[2,128,512]{2,1,0:T(8,128)(2,1)}) custom-call(bf16[128,512]{1,0:T(8,128)(2,1)} %tok_ref.1, bf16[128,512]{1,0:T(8,128)(2,1)} %cot_ref.1), custom_call_target="tpu_custom_call" | custom-call | tf_op jit(solution)/shard_map/pallas_call | solution.py:95
  15.5 14.8 %shard_map.103.part_ref = f32[16,3,16,3584]{3,2,1,0:T(8,128)} custom-call(s32[2,28]{1,0:T(2,128)} %get-tuple-element.13.block_ref, s32[2,28]{1,0:T(2,128)} %get-tuple-element.14.live_ref, bf16[256,512]{1,0:T(8,128)(2,1)} %bitcast.12, bf16[256,512]{1,0:T(8,128)(2,1)} %bitcast.14, bf16[512,7168]{1,0:T(8,128)(2,1)} %refs_6_.3, bf16[512,7168]{1,0:T(8,128)(2,1)} %refs_6_.3, ...), custom_call_target="tpu_custom_call" | custom-call | flops 2818572288 | bytes 22020096 | tf_op jit(solution)/shard_map/pallas_call | solution.py:152
  30.3 117.1 %shard_map.104.act_ref = bf16[16,3,16,3584]{3,2,1,0:T(8,128)(2,1)} custom-call(f32[16,3,16,3584]{3,2,1,0:T(8,128)} %shard_map.103.part_ref), custom_call_target="tpu_custom_call" | custom-call | tf_op jit(solution)/shard_map/pallas_call | solution.py:383
  147.4 14.9 %shard_map.105 = f32[2,2,128,512]{3,2,1,0:T(8,128)} custom-call(s32[2,28]{1,0:T(2,128)} %get-tuple-element.13.block_ref, s32[2,28]{1,0:T(2,128)} %get-tuple-element.14.live_ref, bf16[16,3,16,3584]{3,2,1,0:T(8,128)(2,1)} %shard_map.104.act_ref, bf16[512,7168]{1,0:T(8,128)(2,1)} %refs_6_.3, bf16[512,7168]{1,0:T(8,128)(2,1)} %refs_6_.3, ...), custom_call_target="tpu_custom_call" | custom-call | flops 2818572288 | bytes 22020096 | tf_op jit(solution)/shard_map/pallas_call | solution.py:431
  162.3 0.0 copy-start
  162.3 1.2 fusion.1
  163.5 3.0 %collective-permute-start = (bf16[2,1,128,512]{3,2,0,1:T(8,128)(2,1)S(1)}, bf16[2,1,128,512]{3,2,0,1:T(8,128)(2,1)S(1)}, u32[]{:S(2)}, u32[]{:S(2)}) collective-permute-start(bf16[2,1,128,512]{3,2,0,1:T(8,128)(2,1)S(1)} %fusion.1), channel_id=1, source_target_pairs={{0,1},{1,0},{2,3},{3,2},{4,5},{5,4},{6,7},{7,6},{8,9},{9,8},{10,11... | collective-permute-start | bytes 786440 | tf_op jit(solution)/shard_map/ppermute | solution.py:549
  166.5 18.5 %shard_map.106 = (f32[512,7168]{1,0:T(8,128)}, f32[512,7168]{1,0:T(8,128)}, f32[7168,512]{1,0:T(8,128)}) custom-call(s32[2,56]{1,0:T(2,128)} %get-tuple-element.17.slot_ref, s32[2,56]{1,0:T(2,128)} %mask_ref.3, bf16[256,512]{1,0:T(8,128)(2,1)} %bitcast.13, bf16[256,512]{1,0:T(8,128)(2,1)} %bitcast.15, bf16[16,3,16,3584]{3,2,1,0:T(8,128)(2,1)} %shard_map.104.act_ref), custom_call_target="tpu_custom_call" | custom-call | flops 5637144576 | bytes 44040192 | tf_op jit(solution)/shard_map/pallas_call | solution.py:495
  184.9 0.0 collective-permute-done
  184.9 0.0 copy-done
  184.9 0.1 fusion
  185.0 0.7 slice_bitcast_fusion
Async XLA Ops:
  162.3 22.6 %copy-start = (f32[2,2,128,512]{3,2,1,0:T(8,128)S(1)}, f32[2,2,128,512]{3,2,1,0:T(8,128)}, u32[]{:S(2)}) copy-start(f32[2,2,128,512]{3,2,1,0:T(8,128)} %shard_map.105) | copy-start | bytes 3145732
  163.5 21.5 %collective-permute-start = (bf16[2,1,128,512]{3,2,0,1:T(8,128)(2,1)S(1)}, bf16[2,1,128,512]{3,2,0,1:T(8,128)(2,1)S(1)}, u32[]{:S(2)}, u32[]{:S(2)}) collective-permute-start(bf16[2,1,128,512]{3,2,0,1:T(8,128)(2,1)S(1)} %fusion.1), channel_id=1, source_target_pairs={{0,1},{1,0},{2,3},{3,2},{4,5},{5,4},{6,7},{7,6},{8,9},{9,8},{10,11... | collective-permute-start | bytes 786440 | tf_op jit(solution)/shard_map/ppermute | solution.py:549
